TPU v7x, 256 devices: a whole 4x4x8 slice. The times are simulated.
256 devices in a mesh: expert: 32 (over z, y), etp: 8 (over x, core).
Axes of the slice: x: 4, y: 4, z: 8, core: 2. Of those that a mesh axis runs over, the one named last changes fastest.
Arguments:
- tokens: bfloat16 [32768, 2560], P(('expert', 'etp')), may hold values from -6 to 6
- grad_out: bfloat16 [32768, 2560], P(('expert', 'etp')), may hold values from -6 to 6
- router_weight: bfloat16 [2560, 32], replicated, may hold values from -0.125 to 0.125
- expert_choice: int32 [32768, 1], P(('expert', 'etp')), may hold values from 0 to 31; in each aligned block of 128 rows (0 to 127, 128 to 255, ...) at most 6 rows name the same one
- gate_pre: bfloat16 [32, 1536, 4096], P('expert', None, 'etp'), may hold values from -6 to 6
- up_pre: bfloat16 [32, 1536, 4096], P('expert', None, 'etp'), may hold values from -6 to 6
- w_gate: bfloat16 [32, 2560, 4096], P('expert', None, 'etp'), may hold values from -0.125 to 0.125
- w_up: bfloat16 [32, 2560, 4096], P('expert', None, 'etp'), may hold values from -0.125 to 0.125
- w_down: bfloat16 [32, 4096, 2560], P('expert', 'etp'), may hold values from -0.09375 to 0.09375
Outputs:
- token_grad: bfloat16 [32768, 2560], P(('expert', 'etp'))
- router_grad: float32 [2560, 32], replicated
Inputs may be any that keep to these rules, and one draw needn't show every extreme that they name: `expert_choice`: within the 128 tokens of one device no expert is chosen more than 6 times, and in every draw some expert is chosen exactly 6 times by the tokens of some device.
All inputs are finite; a program needn't handle non-finite values.
Results may differ from a plain program's by a relative error of at most 0.015.
Values may be sent and summed in bfloat16 or wider, within the bound.
No kernel may reach another device: no remote copies, remote signals or barrier semaphores. Data moves between devices by JAX's collectives and lax.ppermute only.
A program may use at most 128 MiB of HBM per device.

v0:
```python
import jax
import jax.numpy as jnp
from jax import lax
from jax.sharding import PartitionSpec as P


def local(tokens, grad_out, router_weight, expert_choice, gate_pre, up_pre, w_gate, w_up, w_down):
    width = tokens.shape[1]
    experts = router_weight.shape[1]
    n_expert = lax.axis_size("expert")
    n_etp = lax.axis_size("etp")
    capacity = gate_pre.shape[1] // (n_expert * n_etp)
    contract = (((1,), (1,)), ((), ()))
    chosen_ids = expert_choice[:, 0]
    picked = chosen_ids[:, None] == jnp.arange(experts, dtype=jnp.int32)[None, :]
    logits = jnp.dot(tokens, router_weight, preferred_element_type=jnp.float32)
    score = jax.nn.sigmoid(jnp.sum(jnp.where(picked, logits, 0.0), axis=1))
    counts = picked.astype(jnp.int32)
    earlier = jnp.cumsum(counts, axis=0) - counts
    position = jnp.sum(earlier * counts, axis=1)
    target = chosen_ids * capacity + position
    placed = jnp.arange(experts * capacity, dtype=jnp.int32)[:, None] == target[None, :]
    onehot = placed.astype(jnp.bfloat16)
    outgoing = jnp.dot(onehot, grad_out, preferred_element_type=jnp.float32).astype(jnp.bfloat16)
    own = lax.all_to_all(outgoing, "expert", split_axis=0, concat_axis=0, tiled=True)
    arrived = lax.all_gather(own, "etp", axis=0, tiled=True)
    d_hidden = lax.dot_general(arrived, w_down[0], contract, preferred_element_type=jnp.float32)
    gate_f = gate_pre[0].astype(jnp.float32)
    up_f = up_pre[0].astype(jnp.float32)
    sig = jax.nn.sigmoid(gate_f)
    d_gate = (d_hidden * up_f * sig * (1.0 + gate_f * (1.0 - sig))).astype(jnp.bfloat16)
    d_up = (d_hidden * gate_f * sig).astype(jnp.bfloat16)
    terms = (
        lax.dot_general(d_gate, w_gate[0], contract, preferred_element_type=jnp.float32)
        + lax.dot_general(d_up, w_up[0], contract, preferred_element_type=jnp.float32)
    ).astype(jnp.bfloat16)
    summed = lax.psum_scatter(terms, "etp", scatter_dimension=0, tiled=True)
    returned = lax.all_to_all(summed, "expert", split_axis=0, concat_axis=0, tiled=True)
    fetched = lax.dot_general(
        onehot, returned, (((0,), (0,)), ((), ())), preferred_element_type=jnp.float32
    )
    inputs = tokens.astype(jnp.float32)
    d_logit = jnp.sum(inputs * fetched, axis=1) * score * (1.0 - score)
    column = lax.dot_general(
        picked.astype(jnp.bfloat16), router_weight, contract, preferred_element_type=jnp.float32
    )
    token_grad = (score[:, None] * fetched + d_logit[:, None] * column).astype(jnp.bfloat16)
    weighted = jnp.where(picked, d_logit[:, None], 0.0)
    local_terms = lax.dot_general(
        weighted,
        inputs,
        (((0,), (0,)), ((), ())),
        precision=lax.Precision.HIGHEST,
        preferred_element_type=jnp.float32,
    )
    mine = lax.all_to_all(
        local_terms.reshape(n_etp, experts // n_etp, width),
        "etp",
        split_axis=0,
        concat_axis=0,
        tiled=True,
    )
    mine = jnp.sum(mine, axis=0)
    mine = lax.psum(mine, "expert")
    router_grad = lax.all_gather(mine, "etp", axis=0, tiled=True).T
    return (token_grad, router_grad)


def solution(mesh):
    placed = (
        P(("expert", "etp"), None),
        P(("expert", "etp"), None),
        P(),
        P(("expert", "etp"), None),
        P("expert", None, "etp"),
        P("expert", None, "etp"),
        P("expert", None, "etp"),
        P("expert", None, "etp"),
        P("expert", "etp", None),
    )
    return jax.shard_map(
        local,
        mesh=mesh,
        in_specs=placed,
        out_specs=(P(("expert", "etp"), None), P()),
        check_vma=False,
    )
```

profile of v0, /device:TPU:1, one launch (start us, length us, event | category | flops | bytes accessed | tf_op | source)
XLA Modules:
  0.0 423.1 jit_solution(13606596880845416231)
XLA Ops:
  7.2 0.0 copy-start
  7.2 0.0 all-gather.3.cloned.1.call-start
  7.2 0.8 fusion.29
  8.0 0.1 copy.15
  8.1 0.2 reduce_window_sum.11
  8.3 0.1 copy.16
  8.4 0.7 select_reduce_fusion
  9.1 0.7 multiply_add_fusion
  9.7 2.5 convolution_convert_fusion
  12.2 2.3 all_to_all.19
  14.4 46.0 %all_to_all.29 = bf16[32,6,2560]{2,1,0:T(8,128)(2,1)} all-to-all(bf16[32,6,2560]{2,1,0:T(8,128)(2,1)} %all_to_all.19), channel_id=1, replica_groups=mesh['expert'=32,'etp'=8] {'expert'}, dimensions={0} | all-to-all | bytes 1966080 | tf_op jit(solution)/shard_map/all_to_all | solution.py:25
  60.4 2.3 all_to_all.21
  62.7 0.0 all-gather.3.cloned.1.call-update
  62.7 0.0 reduce-scatter.2.cloned.1.call-start
  62.8 47.8 %all-gather.3.cloned.1.call-done = bf16[1536,2560]{1,0:T(8,128)(2,1)} async-done(((bf16[192,2560]{1,0:T(8,128)(2,1)}), bf16[1536,2560]{1,0:T(8,128)(2,1)}) %all-gather.3.cloned.1.call-update) | async-done | bytes 7864336 | tf_op jit(solution)/shard_map/all_gather | solution.py:26
  110.6 0.0 copy-start.4
  110.6 0.0 copy-start.5
  110.6 7.5 %fusion.14 = f32[1536,512]{1,0:T(8,128)S(1)} fusion(bf16[1536,2560]{1,0:T(8,128)(2,1)} %all-gather.3.cloned.1.call-done, bf16[1,512,2560]{2,1,0:T(8,128)(2,1)} %param.17), kind=kOutput, calls=%fused_computation.21 | convolution fusion | flops 4026531840 | bytes 13631488 | tf_op jit(solution)/shard_map/dot_general | solution.py:27
  118.1 0.0 copy-start.6
  118.1 1.7 copy-done.6
  119.8 0.0 copy-done
  119.8 0.0 copy-done.4
  119.8 0.0 copy-done.5
  119.8 9.8 %fusion.12 = f32[1536,2560]{1,0:T(8,128)} fusion(bf16[1,2560,512]{2,1,0:T(8,128)(2,1)S(1)} %copy-done, f32[1536,512]{1,0:T(8,128)S(1)} %fusion.14, bf16[1,1536,512]{2,1,0:T(8,128)(2,1)S(1)} %copy-done.4, bf16[1,1536,512]{2,1,0:T(8,128)(2,1)S(1)} %copy-done.5), kind=kOutput, calls=%fused_computation.19 | convolution fusion | flops 4035969024 | bytes 24641536 | tf_op jit(solution)/shard_map/dot_general | solution.py:34
  129.6 15.2 %add_convert_fusion = bf16[1536,2560]{1,0:T(8,128)(2,1)} fusion(f32[1536,2560]{1,0:T(8,128)} %fusion.12, bf16[1,2560,512]{2,1,0:T(8,128)(2,1)} %param.16, f32[1536,512]{1,0:T(8,128)} %copy-done.6, bf16[1,1536,512]{2,1,0:T(8,128)(2,1)} %param.13), kind=kOutput, calls=%fused_computation | convolution fusion | flops 4039901184 | bytes 30932992 | tf_op jit(solution)/shard_map/dot_general | solution.py:35
  144.9 0.0 reduce-scatter.2.cloned.1.call-update
  144.9 0.0 copy-start.1
  144.9 0.0 copy-start.2
  144.9 0.0 copy-start.3
  144.9 51.8 %reduce-scatter.2.cloned.1.call-done = bf16[192,2560]{1,0:T(8,128)(2,1)} async-done(((bf16[1536,2560]{1,0:T(8,128)(2,1)}), bf16[192,2560]{1,0:T(8,128)(2,1)}) %reduce-scatter.2.cloned.1.call-update) | async-done | bytes 983056 | tf_op jit(solution)/shard_map/reduce_scatter | solution.py:37
  196.8 2.3 all_to_all.22
  199.0 9.7 %all-to-all-start.1 = ((bf16[32,6,2560]{2,1,0:T(8,128)(2,1)}), bf16[32,6,2560]{2,1,0:T(8,128)(2,1)}, u32[]{:S(2)}, u32[]{:S(2)}) async-start(bf16[32,6,2560]{2,1,0:T(8,128)(2,1)} %all_to_all.22), calls=%async_computation.2 | async-start | bytes 2621440 | tf_op jit(solution)/shard_map/all_to_all | solution.py:38
  208.7 0.0 copy-done.1
  208.7 0.0 copy-done.2
  208.8 0.0 copy-done.3
  208.8 0.3 fusion.23
  209.1 30.4 %all-to-all-done.1 = bf16[32,6,2560]{2,1,0:T(8,128)(2,1)} async-done(((bf16[32,6,2560]{2,1,0:T(8,128)(2,1)}), bf16[32,6,2560]{2,1,0:T(8,128)(2,1)}, u32[]{:S(2)}, u32[]{:S(2)}) %all-to-all-start.1) | async-done | bytes 983072 | tf_op jit(solution)/shard_map/all_to_all | solution.py:38
  239.5 2.2 all_to_all.24
  241.7 2.7 multiply_reduce_fusion
  244.4 1.1 fusion.27
  245.5 1.8 reshape.36
  247.3 7.3 %all-to-all-start.2 = ((f32[8,4,2560]{2,1,0:T(4,128)}), f32[8,4,2560]{2,1,0:T(4,128)S(1)}, u32[]{:S(2)}, u32[]{:S(2)}) async-start(f32[8,4,2560]{2,1,0:T(4,128)} %reshape.36), calls=%async_computation.3 | async-start | bytes 655360 | tf_op jit(solution)/shard_map/all_to_all | solution.py:56
  254.6 2.5 fusion.1
  257.1 4.6 %all-to-all-done.2 = f32[8,4,2560]{2,1,0:T(4,128)S(1)} async-done(((f32[8,4,2560]{2,1,0:T(4,128)}), f32[8,4,2560]{2,1,0:T(4,128)S(1)}, u32[]{:S(2)}, u32[]{:S(2)}) %all-to-all-start.2) | async-done | bytes 327712 | tf_op jit(solution)/shard_map/all_to_all | solution.py:56
  261.7 0.1 reduce_sum.39
  261.8 112.4 %psum.7 = f32[4,2560]{1,0:T(4,128)S(1)} all-reduce(f32[4,2560]{1,0:T(4,128)S(1)} %reduce_sum.39), channel_id=1, replica_groups=mesh['expert'=32,'etp'=8] {'expert'}, use_global_device_ids=true, to_apply=%region_6.7 | all-reduce | flops 10240 | bytes 81920 | tf_op jit(solution)/shard_map/psum | solution.py:64
  374.2 41.3 %all-gather = f32[8,4,2560]{2,1,0:T(4,128)S(1)} all-gather(f32[1,4,2560]{2,1,0:T(4,128)S(1)} %bitcast.37), channel_id=1, replica_groups=mesh['expert'=32,'etp'=8] {'etp'}, dimensions={0}, use_global_device_ids=true | all-gather | bytes 368640 | tf_op jit(solution)/shard_map/all_gather | solution.py:65
  415.5 0.8 reshape.40
  (1 shorter events, 0.0 us)
Async XLA Ops:
  7.2 112.6 %copy-start = (bf16[1,2560,512]{2,1,0:T(8,128)(2,1)S(1)}, bf16[1,2560,512]{2,1,0:T(8,128)(2,1)}, u32[]{:S(2)}) copy-start(bf16[1,2560,512]{2,1,0:T(8,128)(2,1)} %param.15) | copy-start | bytes 7864324
  7.2 103.4 %all-gather.3.cloned.1.call-start = ((), (), s32[]{:S(2)}) async-start(), calls=%async_computation.4 | async-start | bytes 8847360 | tf_op jit(solution)/shard_map/all_gather | solution.py:26
  62.7 134.0 %reduce-scatter.2.cloned.1.call-start = ((), (), s32[]{:S(2)}) async-start(), calls=%async_computation.5 | async-start | bytes 8847360 | tf_op jit(solution)/shard_map/reduce_scatter | solution.py:37
  110.6 9.3 %copy-start.4 = (bf16[1,1536,512]{2,1,0:T(8,128)(2,1)S(1)}, bf16[1,1536,512]{2,1,0:T(8,128)(2,1)}, u32[]{:S(2)}) copy-start(bf16[1,1536,512]{2,1,0:T(8,128)(2,1)} %param.14) | copy-start | bytes 4718596
  110.6 9.3 %copy-start.5 = (bf16[1,1536,512]{2,1,0:T(8,128)(2,1)S(1)}, bf16[1,1536,512]{2,1,0:T(8,128)(2,1)}, u32[]{:S(2)}) copy-start(bf16[1,1536,512]{2,1,0:T(8,128)(2,1)} %param.13) | copy-start | bytes 4718596
  118.1 1.7 copy-start.6
  144.9 63.8 %copy-start.1 = (bf16[128,2560]{1,0:T(8,128)(2,1)S(1)}, bf16[128,2560]{1,0:T(8,128)(2,1)}, u32[]{:S(2)}) copy-start(bf16[128,2560]{1,0:T(8,128)(2,1)} %param.9) | copy-start | bytes 1966084
  144.9 63.8 %copy-start.2 = (bf16[2560,32]{0,1:T(8,128)(2,1)S(1)}, bf16[2560,32]{0,1:T(8,128)(2,1)}, u32[]{:S(2)}) copy-start(bf16[2560,32]{0,1:T(8,128)(2,1)} %param.11) | copy-start | bytes 491524
  144.9 63.8 %copy-start.3 = (s32[128,1]{0,1:T(1,128)S(1)}, s32[128,1]{0,1:T(1,128)}, u32[]{:S(2)}) copy-start(s32[128,1]{0,1:T(1,128)} %param.12) | copy-start | bytes 1540
  199.0 40.4 %all-to-all-start.1 = ((bf16[32,6,2560]{2,1,0:T(8,128)(2,1)}), bf16[32,6,2560]{2,1,0:T(8,128)(2,1)}, u32[]{:S(2)}, u32[]{:S(2)}) async-start(bf16[32,6,2560]{2,1,0:T(8,128)(2,1)} %all_to_all.22), calls=%async_computation.2 | async-start | bytes 2621440 | tf_op jit(solution)/shard_map/all_to_all | solution.py:38
  247.3 14.4 %all-to-all-start.2 = ((f32[8,4,2560]{2,1,0:T(4,128)}), f32[8,4,2560]{2,1,0:T(4,128)S(1)}, u32[]{:S(2)}, u32[]{:S(2)}) async-start(f32[8,4,2560]{2,1,0:T(4,128)} %reshape.36), calls=%async_computation.3 | async-start | bytes 655360 | tf_op jit(solution)/shard_map/all_to_all | solution.py:56
Sparse Core Ops, SparseCore 0:
  62.9 47.6 all-gather.2
  145.0 51.6 reduce-scatter.1
where the time goes:
time: 424 us; the launch traced here: 423 us
  blocking collectives  200 us (47%)
  waiting for transfers between devices  135 us (32%)
  matrix products  41.7 us (10%)
  starting transfers between devices  17.1 us (4%)
  between operations  14.1 us (3%)
  local copies, waits for them, and re-layouts  13.6 us (3%)
    psum x1, blocking collectives, local(): mine = lax.psum(mine, 'expert')  112 us
    reduce_scatter x1, waiting for transfers between devices, local(): summed = lax.psum_scatter(terms, 'etp', scatter_dimension=0, tiled=True)  51.8 us
    all_gather x1, waiting for transfers between devices, local(): arrived = lax.all_gather(own, 'etp', axis=0, tiled=True)  47.8 us
    all_to_all x1, blocking collectives, local(): lax.all_to_all(outgoing, 'expert', split_axis=0, concat_axis=0, tiled=True)  46 us
    all_gather x1, blocking collectives, local(): router_grad = lax.all_gather(mine, 'etp', axis=0, tiled=True).T  41.3 us
    all_to_all x1, waiting for transfers between devices, local(): lax.all_to_all(summed, 'expert', split_axis=0, concat_axis=0, tiled=True)  30.4 us
    dot_general x1, matrix products, local(): lax.dot_general(d_up, w_up[0], contract, preferred_element_type=jnp.float32)  15.2 us
    dot_general x1, matrix products, local(): lax.dot_general(d_gate, w_gate[0], contract, preferred_element_type=jnp.f...  9.81 us
  transfers between devices with their start and end apart: 4, of which 4 were waited for; matrix products, arithmetic and copies ran while one was open for 1% of the time, Pallas kernels for 0%

commit v1 on v0

--- a/solution.py
+++ b/solution.py
@@ -61,7 +61,7 @@
         tiled=True,
     )
     mine = jnp.sum(mine, axis=0)
-    mine = lax.psum(mine, "expert")
+    mine = jnp.sum(lax.all_gather(mine, "expert"), axis=0)
     router_grad = lax.all_gather(mine, "etp", axis=0, tiled=True).T
     return (token_grad, router_grad)
 

time: 424 us -> 357 us (0.84)
  blocking collectives: 200 us -> 78.7 us
  waiting for transfers between devices: 135 us -> 195 us
  starting transfers between devices: 17.1 us -> 9.81 us
    psum x1 -> x0, blocking collectives: 112 us -> none  [local(): mine = lax.psum(mine, 'expert')]
    all_gather x0 -> x1, waiting for transfers between devices: none -> 64.9 us  [local(): mine = jnp.sum(lax.all_gather(mine, 'expert'), axis=0)]
    all_gather x1, blocking collectives: 41.3 us -> 18.1 us  [local(): router_grad = lax.all_gather(mine, 'etp', axis=0, tiled=True).T]
    all_to_all x0 -> x1, blocking collectives: none -> 14.6 us  [local(): lax.all_to_all(local_terms.reshape(n_etp, experts // n_etp, width), 'etp'...]
    all_to_all x1 -> x0, starting transfers between devices: 7.3 us -> none  [local(): lax.all_to_all(local_terms.reshape(n_etp, experts // n_etp, width), 'etp'...]
    all_to_all x1 -> x0, waiting for transfers between devices: 4.58 us -> none  [local(): lax.all_to_all(local_terms.reshape(n_etp, experts // n_etp, width), 'etp'...]
where the time goes in v1:
time: 357 us; the launch traced here: 356 us
  waiting for transfers between devices  195 us (55%)
  blocking collectives  78.7 us (22%)
  matrix products  41.7 us (12%)
  between operations  13.8 us (4%)
  local copies, waits for them, and re-layouts  12.9 us (4%)
  starting transfers between devices  9.81 us (3%)
  other arithmetic  4.55 us (1%)
    all_gather x1, waiting for transfers between devices, local(): mine = jnp.sum(lax.all_gather(mine, 'expert'), axis=0)  64.9 us
    reduce_scatter x1, waiting for transfers between devices, local(): summed = lax.psum_scatter(terms, 'etp', scatter_dimension=0, tiled=True)  51.8 us
    all_gather x1, waiting for transfers between devices, local(): arrived = lax.all_gather(own, 'etp', axis=0, tiled=True)  47.8 us
    all_to_all x1, blocking collectives, local(): lax.all_to_all(outgoing, 'expert', split_axis=0, concat_axis=0, tiled=True)  46 us
    all_to_all x1, waiting for transfers between devices, local(): lax.all_to_all(summed, 'expert', split_axis=0, concat_axis=0, tiled=True)  30.3 us
    all_gather x1, blocking collectives, local(): router_grad = lax.all_gather(mine, 'etp', axis=0, tiled=True).T  18.1 us
    dot_general x1, matrix products, local(): lax.dot_general(d_up, w_up[0], contract, preferred_element_type=jnp.float32)  15.2 us
    all_to_all x1, blocking collectives, local(): lax.all_to_all(local_terms.reshape(n_etp, experts // n_etp, width), 'etp'...  14.6 us
  transfers between devices with their start and end apart: 4, of which 4 were waited for; matrix products, arithmetic and copies ran while one was open for 1% of the time, Pallas kernels for 0%

profile of v1, /device:TPU:1, one launch (start us, length us, event | category | flops | bytes accessed | tf_op | source)
XLA Modules:
  0.0 356.3 jit_solution(13958498987821106013)
XLA Ops:
  7.2 0.0 copy-start
  7.2 0.0 all-gather.6.cloned.1.call-start
  7.2 0.8 fusion.29
  8.0 0.1 copy.15
  8.1 0.2 reduce_window_sum.11
  8.3 0.1 copy.16
  8.4 0.7 select_reduce_fusion
  9.1 0.7 multiply_add_fusion
  9.7 2.5 convolution_convert_fusion
  12.2 2.3 all_to_all.19
  14.4 46.0 %all_to_all.29 = bf16[32,6,2560]{2,1,0:T(8,128)(2,1)} all-to-all(bf16[32,6,2560]{2,1,0:T(8,128)(2,1)} %all_to_all.19), channel_id=1, replica_groups=mesh['expert'=32,'etp'=8] {'expert'}, dimensions={0} | all-to-all | bytes 1966080 | tf_op jit(solution)/shard_map/all_to_all | solution.py:25
  60.4 2.3 all_to_all.21
  62.7 0.0 all-gather.6.cloned.1.call-update
  62.7 0.0 reduce-scatter.2.cloned.1.call-start
  62.8 47.8 %all-gather.6.cloned.1.call-done = bf16[1536,2560]{1,0:T(8,128)(2,1)} async-done(((bf16[192,2560]{1,0:T(8,128)(2,1)}), bf16[1536,2560]{1,0:T(8,128)(2,1)}) %all-gather.6.cloned.1.call-update) | async-done | bytes 7864336 | tf_op jit(solution)/shard_map/all_gather | solution.py:26
  110.6 7.5 %fusion.14 = f32[1536,512]{1,0:T(8,128)S(1)} fusion(bf16[1536,2560]{1,0:T(8,128)(2,1)} %all-gather.6.cloned.1.call-done, bf16[1,512,2560]{2,1,0:T(8,128)(2,1)} %param.17), kind=kOutput, calls=%fused_computation.21 | convolution fusion | flops 4026531840 | bytes 13631488 | tf_op jit(solution)/shard_map/dot_general | solution.py:27
  118.1 0.0 copy-start.6
  118.1 1.7 copy-done.6
  119.8 0.0 copy-done
  119.8 0.0 copy-done.4
  119.8 0.0 copy-done.5
  119.8 9.8 %fusion.12 = f32[1536,2560]{1,0:T(8,128)} fusion(bf16[1,2560,512]{2,1,0:T(8,128)(2,1)S(1)} %copy-done, f32[1536,512]{1,0:T(8,128)S(1)} %fusion.14, bf16[1,1536,512]{2,1,0:T(8,128)(2,1)S(1)} %copy-done.4, bf16[1,1536,512]{2,1,0:T(8,128)(2,1)S(1)} %copy-done.5), kind=kOutput, calls=%fused_computation.19 | convolution fusion | flops 4035969024 | bytes 24641536 | tf_op jit(solution)/shard_map/dot_general | solution.py:34
  129.6 15.2 %add_convert_fusion = bf16[1536,2560]{1,0:T(8,128)(2,1)} fusion(f32[1536,2560]{1,0:T(8,128)} %fusion.12, bf16[1,2560,512]{2,1,0:T(8,128)(2,1)} %param.16, f32[1536,512]{1,0:T(8,128)} %copy-done.6, bf16[1,1536,512]{2,1,0:T(8,128)(2,1)} %param.13), kind=kOutput, calls=%fused_computation | convolution fusion | flops 4039901184 | bytes 30932992 | tf_op jit(solution)/shard_map/dot_general | solution.py:35
  144.9 0.0 reduce-scatter.2.cloned.1.call-update
  144.9 0.0 copy-start.1
  144.9 0.0 copy-start.2
  144.9 0.0 copy-start.3
  144.9 51.8 %reduce-scatter.2.cloned.1.call-done = bf16[192,2560]{1,0:T(8,128)(2,1)} async-done(((bf16[1536,2560]{1,0:T(8,128)(2,1)}), bf16[192,2560]{1,0:T(8,128)(2,1)}) %reduce-scatter.2.cloned.1.call-update) | async-done | bytes 983056 | tf_op jit(solution)/shard_map/reduce_scatter | solution.py:37
  196.8 2.3 all_to_all.22
  199.0 9.7 %all-to-all-start.1 = ((bf16[32,6,2560]{2,1,0:T(8,128)(2,1)}), bf16[32,6,2560]{2,1,0:T(8,128)(2,1)}, u32[]{:S(2)}, u32[]{:S(2)}) async-start(bf16[32,6,2560]{2,1,0:T(8,128)(2,1)} %all_to_all.22), calls=%async_computation.2 | async-start | bytes 2621440 | tf_op jit(solution)/shard_map/all_to_all | solution.py:38
  208.7 0.0 all-gather.8.cloned.1.call-start
  208.8 0.0 copy-done.1
  208.8 0.0 copy-done.2
  208.8 0.0 copy-done.3
  208.8 0.3 fusion.23
  209.1 30.3 %all-to-all-done.1 = bf16[32,6,2560]{2,1,0:T(8,128)(2,1)} async-done(((bf16[32,6,2560]{2,1,0:T(8,128)(2,1)}), bf16[32,6,2560]{2,1,0:T(8,128)(2,1)}, u32[]{:S(2)}, u32[]{:S(2)}) %all-to-all-start.1) | async-done | bytes 983072 | tf_op jit(solution)/shard_map/all_to_all | solution.py:38
  239.5 2.2 all_to_all.24
  241.7 2.7 multiply_reduce_fusion
  244.4 1.1 fusion.27
  245.5 1.1 reshape.36
  246.5 14.6 %all_to_all.30 = f32[8,4,2560]{2,1,0:T(4,128)S(1)} all-to-all(f32[8,4,2560]{2,1,0:T(4,128)S(1)} %reshape.36), channel_id=1, replica_groups=mesh['expert'=32,'etp'=8] {'etp'}, dimensions={0} | all-to-all | bytes 655360 | tf_op jit(solution)/shard_map/all_to_all | solution.py:56
  261.1 0.7 reduce_sum.48
  261.8 0.0 all-gather.8.cloned.1.call-update
  261.8 2.5 fusion.1
  264.4 64.9 %all-gather.8.cloned.1.call-done = f32[32,4,2560]{2,1,0:T(4,128)} async-done(((f32[1,4,2560]{2,1,0:T(4,128)}), f32[32,4,2560]{2,1,0:T(4,128)}) %all-gather.8.cloned.1.call-update) | async-done | bytes 1310736 | tf_op jit(solution)/shard_map/all_gather | solution.py:64
  329.3 1.5 reduce_sum.49
  330.8 18.1 %all-gather.2 = f32[8,4,2560]{2,1,0:T(4,128)S(1)} all-gather(f32[1,4,2560]{2,1,0:T(4,128)S(1)} %bitcast.38), channel_id=1, replica_groups=mesh['expert'=32,'etp'=8] {'etp'}, dimensions={0}, use_global_device_ids=true | all-gather | bytes 368640 | tf_op jit(solution)/shard_map/all_gather | solution.py:65
  349.0 0.8 reshape.43
  (3 shorter events, 0.0 us)
Async XLA Ops:
  7.2 112.6 %copy-start = (bf16[1,2560,512]{2,1,0:T(8,128)(2,1)S(1)}, bf16[1,2560,512]{2,1,0:T(8,128)(2,1)}, u32[]{:S(2)}) copy-start(bf16[1,2560,512]{2,1,0:T(8,128)(2,1)} %param.15) | copy-start | bytes 7864324
  7.2 103.4 %all-gather.6.cloned.1.call-start = ((), (), s32[]{:S(2)}) async-start(), calls=%async_computation.4 | async-start | bytes 8847360 | tf_op jit(solution)/shard_map/all_gather | solution.py:26
  62.7 134.0 %reduce-scatter.2.cloned.1.call-start = ((), (), s32[]{:S(2)}) async-start(), calls=%async_computation.5 | async-start | bytes 8847360 | tf_op jit(solution)/shard_map/reduce_scatter | solution.py:37
  110.6 9.3 %copy-start.4 = (bf16[1,1536,512]{2,1,0:T(8,128)(2,1)S(1)}, bf16[1,1536,512]{2,1,0:T(8,128)(2,1)}, u32[]{:S(2)}) copy-start(bf16[1,1536,512]{2,1,0:T(8,128)(2,1)} %param.14) | copy-start | bytes 4718596
  110.6 9.3 %copy-start.5 = (bf16[1,1536,512]{2,1,0:T(8,128)(2,1)S(1)}, bf16[1,1536,512]{2,1,0:T(8,128)(2,1)}, u32[]{:S(2)}) copy-start(bf16[1,1536,512]{2,1,0:T(8,128)(2,1)} %param.13) | copy-start | bytes 4718596
  118.1 1.7 copy-start.6
  144.9 63.9 %copy-start.1 = (bf16[128,2560]{1,0:T(8,128)(2,1)S(1)}, bf16[128,2560]{1,0:T(8,128)(2,1)}, u32[]{:S(2)}) copy-start(bf16[128,2560]{1,0:T(8,128)(2,1)} %param.9) | copy-start | bytes 1966084
  144.9 63.9 %copy-start.2 = (bf16[2560,32]{0,1:T(8,128)(2,1)S(1)}, bf16[2560,32]{0,1:T(8,128)(2,1)}, u32[]{:S(2)}) copy-start(bf16[2560,32]{0,1:T(8,128)(2,1)} %param.11) | copy-start | bytes 491524
  144.9 63.9 %copy-start.3 = (s32[128,1]{0,1:T(1,128)S(1)}, s32[128,1]{0,1:T(1,128)}, u32[]{:S(2)}) copy-start(s32[128,1]{0,1:T(1,128)} %param.12) | copy-start | bytes 1540
  199.0 40.4 %all-to-all-start.1 = ((bf16[32,6,2560]{2,1,0:T(8,128)(2,1)}), bf16[32,6,2560]{2,1,0:T(8,128)(2,1)}, u32[]{:S(2)}, u32[]{:S(2)}) async-start(bf16[32,6,2560]{2,1,0:T(8,128)(2,1)} %all_to_all.22), calls=%async_computation.2 | async-start | bytes 2621440 | tf_op jit(solution)/shard_map/all_to_all | solution.py:38
  208.7 120.6 %all-gather.8.cloned.1.call-start = ((), (), s32[]{:S(2)}) async-start(), calls=%async_computation.6 | async-start | bytes 1351680 | tf_op jit(solution)/shard_map/all_gather | solution.py:64
Sparse Core Ops, SparseCore 0:
  62.9 47.6 all-gather.5
  145.0 51.6 reduce-scatter.1
  262.0 67.2 all-gather.7
